TPU v7x, 32 devices: a whole 2x2x4 slice. The times are simulated.
32 devices in a mesh: replica: 4 (over y, x), shard: 8 (over z, core).
Axes of the slice: x: 2, y: 2, z: 4, core: 2. Of those that a mesh axis runs over, the one named last changes fastest.
Arguments:
- tokens: bfloat16 [4096, 4096], P(('replica', 'shard')), parts along dimension 0, may hold values from -6 to 6
- queries: bfloat16 [4096, 2048], P(('replica', 'shard')), parts along dimension 0, may hold values from -48 to 48
- values: bfloat16 [4096, 512], P(('replica', 'shard')), parts along dimension 0, may hold values from -6 to 6
- out_grad: bfloat16 [4096, 2048], P(('replica', 'shard')), parts along dimension 0, may hold values from -6 to 6
- w_key: bfloat16 [16384, 512], P(('replica', 'shard')), parts along dimension 0, may hold values from -0.09375 to 0.09375
- norm_gain: bfloat16 [16384], P(('replica', 'shard')), parts along dimension 0, may hold values from 0.5 to 1.5
- key_momentum: float32 [16384, 512], P(('replica', 'shard')), parts along dimension 0, may hold values from -6 to 6
- gain_momentum: float32 [16384], P(('replica', 'shard')), parts along dimension 0, may hold values from -6 to 6
Outputs:
- attended: bfloat16 [4096, 2048], P(('replica', 'shard')), parts along dimension 0
- new_key_weight: bfloat16 [16384, 512], P(('replica', 'shard')), parts along dimension 0
- new_key_momentum: float32 [16384, 512], P(('replica', 'shard')), parts along dimension 0
- new_gain: bfloat16 [16384], P(('replica', 'shard')), parts along dimension 0
- new_gain_momentum: float32 [16384], P(('replica', 'shard')), parts along dimension 0
There are 4 independent parts, one for each index of `replica`. A program takes and returns all parts, laid end to end along the dimension named above; each array names one. Nothing has to cross between parts.
All inputs are finite; a program needn't handle non-finite values.
Results may differ from a plain program's by a relative error of at most 0.02.
Values may be sent and summed in bfloat16 or wider, within the bound.
No kernel may reach another device: no remote copies, remote signals or barrier semaphores. Data moves between devices by JAX's collectives and lax.ppermute only.
A program may use at most 128 MiB of HBM per device.

v0:
```python
import math
import jax
import jax.numpy as jnp
from jax import lax
from jax.sharding import PartitionSpec as P

HD = 128
epsilon = 1e-05
rope_base = 500000.0
inertia = 0.9
step_size = 0.01


def rotation_tables(positions, head_width):
    half_width = head_width // 2
    exponent = jnp.arange(half_width, dtype=jnp.float32) * (2.0 / head_width)
    frequency = jnp.exp(-math.log(rope_base) * exponent)
    angles = positions.astype(jnp.float32)[:, None] * frequency[None, :]
    return (jnp.cos(angles)[:, None, :], jnp.sin(angles)[:, None, :])


def rotate_keys(raw_rows, cosine, sine_table):
    first_half, second_half = jnp.split(raw_rows, 2, axis=-1)
    return jnp.concatenate(
        [
            first_half * cosine - second_half * sine_table,
            second_half * cosine + first_half * sine_table,
        ],
        axis=-1,
    )


def rotate_back(grad_rows, cosine, sine_table):
    first_half, second_half = jnp.split(grad_rows, 2, axis=-1)
    return jnp.concatenate(
        [
            first_half * cosine + second_half * sine_table,
            second_half * cosine - first_half * sine_table,
        ],
        axis=-1,
    )


def shards(tokens, queries, values, out_grad, w_key, norm_gain, key_momentum, gain_momentum):
    token_rows, model_width = tokens.shape
    key_width = w_key.shape[1]
    head_width = HD
    key_heads = key_width // head_width
    group_size = queries.shape[1] // key_width
    score_scale = head_width ** (-0.5)
    my_index = lax.axis_index("shard")
    first_token = my_index * token_rows
    last_token = first_token + token_rows - 1
    positions = first_token + jnp.arange(token_rows, dtype=jnp.int32)
    cosine, sine_table = rotation_tables(positions, head_width)
    inputs_float = tokens.astype(jnp.float32)
    inverse_rms = lax.rsqrt(jnp.mean(inputs_float * inputs_float, axis=1, keepdims=True) + epsilon)
    normalized = inputs_float * inverse_rms
    weight_rows = lax.all_gather(w_key, "shard", axis=0, tiled=True)
    gain_rows = lax.all_gather(norm_gain, "shard", axis=0, tiled=True)
    scaled = (normalized * gain_rows.astype(jnp.float32)[None, :]).astype(jnp.bfloat16)
    key_sum = jnp.dot(scaled, weight_rows, preferred_element_type=jnp.float32)
    key_local = rotate_keys(key_sum.reshape(token_rows, key_heads, head_width), cosine, sine_table)
    key_local = key_local.reshape(token_rows, key_width).astype(jnp.bfloat16)
    all_keys, all_values = (
        lax.all_gather(key_local, "shard", axis=0, tiled=True),
        lax.all_gather(values, "shard", axis=0, tiled=True),
    )
    total_tokens = all_keys.shape[0]
    query_heads = queries.reshape(token_rows, key_heads, group_size, head_width)
    grad_heads = out_grad.reshape(token_rows, key_heads, group_size, head_width)

    def block_scores(block_keys, block_begin):
        scores = (
            jnp.einsum(
                "tghd,sgd->ghts", query_heads, block_keys, preferred_element_type=jnp.float32
            )
            * score_scale
        )
        key_pos = block_begin + jnp.arange(block_keys.shape[0], dtype=jnp.int32)
        allowed = key_pos[None, :] <= positions[:, None]
        return jnp.where(allowed[None, None], scores, -jnp.inf)

    block_width = math.gcd(total_tokens, 512)
    block_total = total_tokens // block_width
    key_blocks = all_keys.reshape(block_total, block_width, key_heads, head_width)
    value_blocks = all_values.reshape(block_total, block_width, key_heads, head_width)
    block_starts = jnp.arange(block_total, dtype=jnp.int32) * block_width

    def max_pass(running, inputs):
        block_keys, block_begin = inputs

        def live_max():
            return jnp.maximum(running, jnp.max(block_scores(block_keys, block_begin), axis=-1))

        return (lax.cond(block_begin <= last_token, live_max, lambda: running), None)

    max_start = jnp.full((key_heads, group_size, token_rows), -jnp.inf, jnp.float32)
    row_max, unused = lax.scan(max_pass, max_start, (key_blocks, block_starts))

    def sum_pass(running, inputs):
        block_keys, block_values, block_begin = inputs

        def live_sum():
            denominator, numerator = running
            weights = jnp.exp(block_scores(block_keys, block_begin) - row_max[..., None])
            denominator = denominator + jnp.sum(weights, axis=-1)
            numerator = numerator + jnp.einsum(
                "ghts,sgd->tghd",
                weights.astype(jnp.bfloat16),
                block_values,
                preferred_element_type=jnp.float32,
            )
            return (denominator, numerator)

        return (lax.cond(block_begin <= last_token, live_sum, lambda: running), None)

    sum_start = (
        jnp.zeros((key_heads, group_size, token_rows), jnp.float32),
        jnp.zeros((token_rows, key_heads, group_size, head_width), jnp.float32),
    )
    (denominator, numerator), unused = lax.scan(
        sum_pass, sum_start, (key_blocks, value_blocks, block_starts)
    )
    attended_full = numerator / jnp.transpose(denominator, (2, 0, 1))[..., None]
    attended = attended_full.reshape(token_rows, key_width * group_size).astype(jnp.bfloat16)
    delta_rows = jnp.einsum("tghd,tghd->ght", grad_heads.astype(jnp.float32), attended_full)
    row_count = lax.axis_size("shard") * token_rows
    inner_width = math.gcd(row_count, 512)
    inner_total = row_count // inner_width

    def one_block(counter):
        begin_here = counter * inner_width

        def live_term():
            block_keys = lax.dynamic_slice_in_dim(all_keys, begin_here, inner_width, 0).reshape(
                inner_width, key_heads, head_width
            )
            block_values = lax.dynamic_slice_in_dim(all_values, begin_here, inner_width, 0).reshape(
                inner_width, key_heads, head_width
            )
            probs = (
                jnp.exp(block_scores(block_keys, begin_here) - row_max[..., None])
                / denominator[..., None]
            )
            prob_grad = jnp.einsum(
                "tghd,sgd->ghts", grad_heads, block_values, preferred_element_type=jnp.float32
            )
            score_grad = (probs * (prob_grad - delta_rows[..., None])).astype(jnp.bfloat16)
            return (
                jnp.einsum(
                    "ghts,tghd->sgd", score_grad, query_heads, preferred_element_type=jnp.float32
                )
                * score_scale
            )

        def empty_term():
            return jnp.zeros((inner_width, key_heads, head_width), jnp.float32)

        return lax.cond(begin_here <= last_token, live_term, empty_term)

    block_terms = lax.map(one_block, jnp.arange(inner_total, dtype=jnp.int32))
    key_grads = lax.psum_scatter(
        block_terms.reshape(row_count, key_width).astype(jnp.bfloat16),
        "shard",
        scatter_dimension=0,
        tiled=True,
    ).astype(jnp.float32)
    raw_grads = rotate_back(
        key_grads.reshape(token_rows, key_heads, head_width), cosine, sine_table
    )
    raw_grads = raw_grads.reshape(token_rows, key_width).astype(jnp.bfloat16)
    columns = lax.all_to_all(normalized, "shard", split_axis=1, concat_axis=0, tiled=True)
    normed_columns = (columns * norm_gain.astype(jnp.float32)[None, :]).astype(jnp.bfloat16)
    grad_block = lax.all_gather(raw_grads, "shard", axis=0, tiled=True)
    weight_sum = jnp.einsum(
        "td,tk->dk", normed_columns, grad_block, preferred_element_type=jnp.float32
    )
    normed_grad = jnp.einsum("tk,dk->td", grad_block, w_key, preferred_element_type=jnp.float32)
    gain_sum = jnp.sum(normed_grad * columns, axis=0)
    new_key_momentum = inertia * key_momentum + weight_sum
    new_key_weight = (w_key.astype(jnp.float32) - step_size * new_key_momentum).astype(jnp.bfloat16)
    new_gain_momentum = inertia * gain_momentum + gain_sum
    new_gain = (norm_gain.astype(jnp.float32) - step_size * new_gain_momentum).astype(jnp.bfloat16)
    return (attended, new_key_weight, new_key_momentum, new_gain, new_gain_momentum)


def solution(mesh):
    in_specs = (
        P(("replica", "shard"), None),
        P(("replica", "shard"), None),
        P(("replica", "shard"), None),
        P(("replica", "shard"), None),
        P(("replica", "shard"), None),
        P(("replica", "shard")),
        P(("replica", "shard"), None),
        P(("replica", "shard")),
    )
    out_specs = (
        P(("replica", "shard"), None),
        P(("replica", "shard"), None),
        P(("replica", "shard"), None),
        P(("replica", "shard")),
        P(("replica", "shard")),
    )
    return jax.shard_map(shards, mesh=mesh, in_specs=in_specs, out_specs=out_specs, check_vma=False)
```

profile of v0, /device:TPU:0, one launch (start us, length us, event | category | flops | bytes accessed | tf_op | source)
XLA Modules:
  0.0 247.0 jit_solution(13793263313454300019)
XLA Ops:
  7.2 0.7 all-gather.6.cloned.1.call-update
  7.9 1.7 copy.48
  9.7 0.7 reshape.223
  10.4 14.5 %all-gather = bf16[8,1,512]{2,1,0:T(2,128)(2,1)S(1)} all-gather(bf16[1,1,512]{2,1,0:T(2,128)(2,1)S(1)} %reshape.223), channel_id=1, replica_groups=mesh['replica'=4,'shard'=8] {'shard'}, dimensions={0}, use_global_device_ids=true | all-gather | bytes 9216 | tf_op jit(solution)/shard_map/all_gather | solution.py:60
  24.9 1.5 fusion.46
  26.7 32.5 %all-gather.6.cloned.1.call-done = bf16[4096,512]{1,0:T(8,128)(2,1)} async-done(((bf16[512,512]{1,0:T(8,128)(2,1)}), bf16[4096,512]{1,0:T(8,128)(2,1)}) %all-gather.6.cloned.1.call-update) | async-done | bytes 4194320 | tf_op jit(solution)/shard_map/all_gather | solution.py:59
  59.2 3.3 %fusion.49 = f32[128,512]{1,0:T(8,128)S(1)} fusion(bf16[4096,512]{1,0:T(8,128)(2,1)} %all-gather.6.cloned.1.call-done, f32[4096]{0:T(1024)S(1)} %bitcast.166, bf16[128,4096]{1,0:T(8,128)(2,1)} %param.20, f32[128]{0:T(128)S(1)} %add_rsqrt_fusion), kind=kOutput, calls=%fused_computation.64 | convolution fusion | flops 538968064 | bytes 5521920 | tf_op jit(solution)/shard_map/dot_general | solution.py:62
  63.1 0.8 copy.44
  65.0 1.0 copy.56
  66.0 18.1 %all-gather.10.cloned.1.call-done = bf16[1024,512]{0,1:T(8,128)(2,1)} async-done(((bf16[128,512]{0,1:T(8,128)(2,1)}), bf16[1024,512]{0,1:T(8,128)(2,1)}) %all-gather.10.cloned.1.call-update) | async-done | bytes 1048592 | tf_op jit(solution)/shard_map/all_gather | solution.py:67
  84.1 1.8 reshape.217
  85.9 2.0 copy.51
  87.9 21.0 %all-gather.8.cloned.1.call-done = bf16[1024,512]{0,1:T(8,128)(2,1)} async-done(((bf16[128,512]{0,1:T(8,128)(2,1)}), bf16[1024,512]{0,1:T(8,128)(2,1)}) %all-gather.8.cloned.1.call-update) | async-done | bytes 1048592 | tf_op jit(solution)/shard_map/all_gather | solution.py:66
  108.9 1.8 reshape.215
  110.8 0.9 copy.49
  111.7 4.1 %while.38 = (s32[]{:T(128)}, f32[4,4,128]{2,1,0:T(4,128)S(1)}, s32[2]{0:T(128)S(1)}, s32[]{:T(128)}, bf16[2,512,4,128]{3,1,2,0:T(8,128)(2,1)S(1)}, /*index=5*/bf...) while((s32[]{:T(128)}, f32[4,4,128]{2,1,0:T(4,128)S(1)}, s32[2]{0:T(128)S(1)}, s32[]{:T(128)}, ...), condition=%wide.region_5.6_spmd.clone, body=%wide.region_1.5_spmd.clone.sunk | while | flops 271647360 | bytes 1218747 | solution.py:99
  111.7 0.6 dynamic_slice.60
  113.0 1.6 conditional.9
  113.0 0.7 iota_add_fusion
  113.8 0.7 fusion.6
  115.8 1.0 copy-done.5
  116.9 7.1 %while.39 = (s32[]{:T(128)}, f32[4,4,128]{2,1,0:T(4,128)S(1)}, f32[128,4,4,128]{3,0,2,1:T(8,128)S(1)}, s32[2]{0:T(128)S(1)}, s32[]{:T(128)}, /*index=5*/bf16[2,5...) while((s32[]{:T(128)}, f32[4,4,128]{2,1,0:T(4,128)S(1)}, ...), condition=%wide.region_10.11_spmd.clone, body=%wide.region_6.10_spmd.clone.sunk | while | flops 545587840 | bytes 16505639 | solution.py:122
  118.2 4.6 %conditional.10 = ((f32[4,4,128]{2,1,0:T(4,128)S(1)}, f32[128,4,4,128]{3,0,2,1:T(8,128)S(1)})) conditional(s32[]{:T(128)} %convert_element_type.125, (f32[4,4,128]{2,1,0:T(4,128)S(1)}, f32[128,4,4,128]{3,0,2,1:T(8,128)S(1)}) %tuple.114, (s32[]{:T(128)}, s32[]{:T(128)}, bf16[2,512,4,128]{3,1,2,0:T(8,128)(2,1)}, s32[]{:T(128)}, ...), branch_computations={%region_7.7_spmd, %region_8.9_spmd} | conditional | flops 545587840 | bytes 16504896 | solution.py:116
  118.2 0.7 iota_add_fusion.1
  119.1 2.1 fusion.13
  121.2 1.5 fusion.23
  124.1 1.5 fusion.51
  125.5 1.6 copy.70
  127.3 12.9 %while.40 = (s32[]{:T(128)}, bf16[2,512,4,128]{3,1,2,0:T(8,128)(2,1)}, s32[2]{0:T(128)S(1)}, s32[]{:T(128)}, bf16[1024,512]{0,1:T(8,128)(2,1)}, /*index=5*/bf16[...) while((s32[]{:T(128)}, ...), condition=%wide.region_14.15_spmd.clone, body=%wide.region_11.14_spmd.clone.sunk | while | flops 813236864 | bytes 16939852 | solution.py:162
  128.5 8.5 %conditional.11 = (bf16[1,512,4,128]{3,1,2,0:T(8,128)(2,1)S(1)}) conditional(s32[]{:T(128)} %convert_element_type.126, () %tuple.117, (s32[]{:T(128)}, s32[]{:T(128)}, bf16[1024,512]{0,1:T(8,128)(2,1)}, bf16[128,4,4,128]{3,0,2,1:T(8,128)(2,1)S(1)}, f32[4,4,128]{2,1,0:T(4,128)S(1)}, /*index=5*/f32[4,4,128]{2,1,0:T(4,128)S(1)}, ...), branch_computations={%region_12.12_spmd, %region_13.13_spmd} | conditional | flops 813236864 | bytes 15890002 | solution.py:160
  128.6 1.6 constant_dynamic-slice_fusion
  130.2 2.7 %fusion.53 = f32[4,512,128,4]{2,1,3,0:T(8,128)} fusion(bf16[512,4,128,1]{0,2,3,1:T(8,128)(2,1)S(1)} %bitcast.154, bf16[128,4,4,128]{3,0,2,1:T(8,128)(2,1)S(1)} %get-tuple-element.277), kind=kOutput, calls=%fused_computation.87 | convolution fusion | flops 268435456 | bytes 5242880 | tf_op jit(solution)/shard_map/while/body/eval_jaxpr/cond/branch_1_fun/tghd,sgd->ghts/dot_general | solution.py:75
  133.1 4.0 %fusion.43 = bf16[1,512,4,128]{3,1,2,0:T(8,128)(2,1)S(1)} fusion(bf16[128,4,4,128]{3,0,2,1:T(8,128)(2,1)S(1)} %get-tuple-element.277, f32[4,512,128,4]{2,1,3,0:T(8,128)} %fusion.53, bf16[512,4,128,1]{0,2,3,1:T(8,128)(2,1)S(1)} %bitcast.155, bf16[128,4,4,128]{3,0,2,1:T(8,128)(2,1)S(1)} %copy-done.8, f32[4,4,128]{2,1,0:T(4,128)S(1)} %get-tuple-element.282, ...), kind=kOutput, calls=%fused_computation.45 | convolution fusion | flops 544735232 | bytes 6381568 | tf_op jit(solution)/shard_map/while/body/eval_jaxpr/cond/branch_1_fun/ghts,tghd->sgd/dot_general | solution.py:151
  137.1 0.9 constant_dynamic-update-slice_fusion.2
  139.3 0.8 constant_dynamic-update-slice_fusion.2
  140.1 2.1 copy.57
  142.3 1.2 copy.83
  143.7 1.6 copy.82
  145.3 18.3 %all-to-all-start = ((f32[128,8,512]{2,0,1:T(8,128)}), f32[128,8,512]{2,0,1:T(8,128)S(1)}, u32[]{:S(2)}, u32[]{:S(2)}) async-start(f32[128,8,512]{2,0,1:T(8,128)} %bitcast.156), calls=%async_computation | async-start | bytes 4194304 | tf_op jit(solution)/shard_map/all_to_all | solution.py:173
  163.8 32.9 %reduce-scatter.2.cloned.1.call-done = bf16[128,512]{1,0:T(8,128)(2,1)} async-done(((bf16[1024,512]{1,0:T(8,128)(2,1)}), bf16[128,512]{1,0:T(8,128)(2,1)}) %reduce-scatter.2.cloned.1.call-update) | async-done | bytes 131088 | tf_op jit(solution)/shard_map/reduce_scatter | solution.py:163
  196.7 1.0 reshape.222
  198.2 0.7 copy.84
  198.9 30.5 %all-to-all-done = f32[128,8,512]{2,0,1:T(8,128)S(1)} async-done(((f32[128,8,512]{2,0,1:T(8,128)}), f32[128,8,512]{2,0,1:T(8,128)S(1)}, u32[]{:S(2)}, u32[]{:S(2)}) %all-to-all-start) | async-done | bytes 2097184 | tf_op jit(solution)/shard_map/all_to_all | solution.py:173
  229.4 1.3 fusion.47
  230.7 1.2 copy.52
  231.9 2.2 convert_element_type.77
  234.2 2.0 fusion.48
  236.7 3.8 %subtract_convert_fusion = (bf16[512,512]{1,0:T(8,128)(2,1)}, f32[512,512]{1,0:T(8,128)}) fusion(bf16[512,512]{1,0:T(8,128)(2,1)S(1)} %copy-done.1, bf16[1024,512]{1,0:T(8,128)(2,1)} %fusion.47, bf16[1024,512]{1,0:T(8,128)(2,1)} %all-gather.12.cloned.1.call-done, f32[512,512]{1,0:T(8,128)} %param.26), kind=kOutput, calls=%fused_computation.67 | convolution fusion | flops 538443776 | bytes 5242880 | tf_op jit(solution)/shard_map/td,tk->dk/dot_general | solution.py:176
  (78 shorter events, 7.6 us)
Async XLA Ops:
  7.2 52.0 %all-gather.6.cloned.1.call-start = ((), (), s32[]{:S(2)}) async-start(), calls=%async_computation.2 | async-start | bytes 4718592 | tf_op jit(solution)/shard_map/all_gather | solution.py:59
  7.9 76.2 %all-gather.10.cloned.1.call-start = ((), (), s32[]{:S(2)}) async-start(), calls=%async_computation.4 | async-start | bytes 1179648 | tf_op jit(solution)/shard_map/all_gather | solution.py:67
  9.6 99.3 %all-gather.8.cloned.1.call-start = ((), (), s32[]{:S(2)}) async-start(), calls=%async_computation.3 | async-start | bytes 1179648 | tf_op jit(solution)/shard_map/all_gather | solution.py:66
  26.4 37.7 %copy-start.6 = (bf16[128,2048]{1,0:T(8,128)(2,1)S(1)}, bf16[128,2048]{1,0:T(8,128)(2,1)}, u32[]{:S(2)}) copy-start(bf16[128,2048]{1,0:T(8,128)(2,1)} %param.21) | copy-start | bytes 1572868
  59.2 5.5 %copy-start.7 = (bf16[128,2048]{1,0:T(8,128)(2,1)S(1)}, bf16[128,2048]{1,0:T(8,128)(2,1)}, u32[]{:S(2)}) copy-start(bf16[128,2048]{1,0:T(8,128)(2,1)} %param.23) | copy-start | bytes 1572868
  63.9 132.8 %reduce-scatter.2.cloned.1.call-start = ((), (), s32[]{:S(2)}) async-start(), calls=%async_computation.5 | async-start | bytes 1179648 | tf_op jit(solution)/shard_map/reduce_scatter | solution.py:163
  115.8 1.0 copy-start.5
  118.2 3.0 %copy-start.4 = (bf16[2,512,4,128]{3,1,2,0:T(8,128)(2,1)S(1)}, bf16[2,512,4,128]{3,1,2,0:T(8,128)(2,1)}, u32[]{:S(2)}) copy-start(bf16[2,512,4,128]{3,1,2,0:T(8,128)(2,1)} %get-tuple-element.260) | copy-start | bytes 3145732 | tf_op jit(solution)/shard_map/while/body/eval_jaxpr/cond
  124.1 3.2 %copy-start = (bf16[1024,512]{0,1:T(8,128)(2,1)S(1)}, bf16[1024,512]{0,1:T(8,128)(2,1)}, u32[]{:S(2)}) copy-start(bf16[1024,512]{0,1:T(8,128)(2,1)} %all-gather.10.cloned.1.call-done) | copy-start | bytes 3145732
  128.6 4.5 %copy-start.8 = (bf16[128,4,4,128]{3,0,2,1:T(8,128)(2,1)S(1)}, bf16[128,4,4,128]{3,0,2,1:T(8,128)(2,1)}, u32[]{:S(2)}) copy-start(bf16[128,4,4,128]{3,0,2,1:T(8,128)(2,1)} %get-tuple-element.281) | copy-start | bytes 1572868 | tf_op jit(solution)/shard_map/while/body/eval_jaxpr/cond
  140.1 3.3 %copy-start.2 = (bf16[128,4096]{1,0:T(8,128)(2,1)S(1)}, bf16[128,4096]{1,0:T(8,128)(2,1)}, u32[]{:S(2)}) copy-start(bf16[128,4096]{1,0:T(8,128)(2,1)} %param.20) | copy-start | bytes 3145732
  145.3 53.7 %copy-start.9 = (bf16[512]{0:T(512)(128)(2,1)S(1)}, bf16[512]{0:T(512)(128)(2,1)}, u32[]{:S(2)}) copy-start(bf16[512]{0:T(512)(128)(2,1)} %param.25) | copy-start | bytes 3076
  145.3 85.5 %copy-start.3 = (bf16[128,4,4,128]{3,0,2,1:T(8,128)(2,1)S(1)}, bf16[128,4,4,128]{3,0,2,1:T(8,128)(2,1)}, u32[]{:S(2)}) copy-start(bf16[128,4,4,128]{3,0,2,1:T(8,128)(2,1)} %get-tuple-element.556) | copy-start | bytes 1572868
  145.3 84.2 %all-to-all-start = ((f32[128,8,512]{2,0,1:T(8,128)}), f32[128,8,512]{2,0,1:T(8,128)S(1)}, u32[]{:S(2)}, u32[]{:S(2)}) async-start(f32[128,8,512]{2,0,1:T(8,128)} %bitcast.156), calls=%async_computation | async-start | bytes 4194304 | tf_op jit(solution)/shard_map/all_to_all | solution.py:173
  163.5 70.6 %copy-start.1 = (bf16[512,512]{1,0:T(8,128)(2,1)S(1)}, bf16[512,512]{1,0:T(8,128)(2,1)}, u32[]{:S(2)}) copy-start(bf16[512,512]{1,0:T(8,128)(2,1)} %param.24) | copy-start | bytes 1572868
  163.5 70.6 %all-gather.12.cloned.1.call-start = ((), (), s32[]{:S(2)}) async-start(), calls=%async_computation.6 | async-start | bytes 1179648 | tf_op jit(solution)/shard_map/all_gather | solution.py:175
  198.9 37.2 %copy-start.10 = (f32[512]{0:T(512)S(1)}, f32[512]{0:T(512)}, u32[]{:S(2)}) copy-start(f32[512]{0:T(512)} %param.27) | copy-start | bytes 6148
Sparse Core Ops, SparseCore 0:
  9.6 49.5 all-gather.5
  61.4 22.6 all-gather.9
  86.2 22.6 all-gather.7
  143.5 53.1 reduce-scatter.1
  199.0 27.4 all-gather.11
where the time goes:
time: 248 us; the launch traced here: 247 us
  waiting for transfers between devices  136 us (55%)
  local copies, waits for them, and re-layouts  31.2 us (13%)
  matrix products  20.1 us (8%)
  starting transfers between devices  18.9 us (8%)
  blocking collectives  14.5 us (6%)
  between operations  14.1 us (6%)
  other arithmetic  8.36 us (3%)
  loops' own time  4.27 us (2%)
    reduce_scatter x1, waiting for transfers between devices, shards(): lax.psum_scatter(block_terms.reshape(row_count, key_width).astype(jnp.bfl...  32.9 us
    all_gather x1, waiting for transfers between devices, shards(): weight_rows = lax.all_gather(w_key, 'shard', axis=0, tiled=True)  32.5 us
    all_to_all x1, waiting for transfers between devices, shards(): lax.all_to_all(normalized, 'shard', split_axis=1, concat_axis=0, tiled=True)  30.5 us
    all_gather x1, waiting for transfers between devices, shards(): lax.all_gather(key_local, 'shard', axis=0, tiled=True)  21 us
    all_to_all x1, starting transfers between devices, shards(): lax.all_to_all(normalized, 'shard', split_axis=1, concat_axis=0, tiled=True)  18.3 us
    all_gather x1, waiting for transfers between devices, shards(): lax.all_gather(values, 'shard', axis=0, tiled=True)  18.1 us
    all_gather x1, blocking collectives, shards(): gain_rows = lax.all_gather(norm_gain, 'shard', axis=0, tiled=True)  14.5 us
    unnamed x29, local copies, waits for them, and re-layouts  11.5 us
  transfers between devices with their start and end apart: 6, of which 5 were waited for; matrix products, arithmetic and copies ran while one was open for 9% of the time, Pallas kernels for 0%

commit v1 on v0

--- a/solution.py
+++ b/solution.py
@@ -9,6 +9,17 @@
 rope_base = 500000.0
 inertia = 0.9
 step_size = 0.01
+
+
+def turned_line(value, axis, along):
+    size = lax.axis_size(axis)
+    forward = [(i, (i + 1) % size) for i in range(size)]
+    parts = [value]
+    for reach in range(1, size):
+        parts = [lax.ppermute(parts[0], axis, forward), *parts]
+    whole = jnp.concatenate(parts, axis=along)
+    shift = (lax.axis_index(axis) + 1) * parts[-1].shape[along]
+    return jnp.roll(whole, shift, axis=along)
 
 
 def rotation_tables(positions, head_width):
@@ -56,7 +67,7 @@
     inputs_float = tokens.astype(jnp.float32)
     inverse_rms = lax.rsqrt(jnp.mean(inputs_float * inputs_float, axis=1, keepdims=True) + epsilon)
     normalized = inputs_float * inverse_rms
-    weight_rows = lax.all_gather(w_key, "shard", axis=0, tiled=True)
+    weight_rows = turned_line(w_key, "shard", 0)
     gain_rows = lax.all_gather(norm_gain, "shard", axis=0, tiled=True)
     scaled = (normalized * gain_rows.astype(jnp.float32)[None, :]).astype(jnp.bfloat16)
     key_sum = jnp.dot(scaled, weight_rows, preferred_element_type=jnp.float32)

time: 248 us -> 267 us (1.077)
  waiting for transfers between devices: 136 us -> 145 us
  local copies, waits for them, and re-layouts: 31.2 us -> 35.2 us
  starting transfers between devices: 18.9 us -> 22.5 us
    ppermute x0 -> x7, waiting for transfers between devices: none -> 65.1 us  [turned_line(): parts = [lax.ppermute(parts[0], axis, forward), *parts]]
    all_gather x1 -> x0, waiting for transfers between devices: 32.5 us -> none  [shards(): weight_rows = lax.all_gather(w_key, 'shard', axis=0, tiled=True)]
    all_gather x1, waiting for transfers between devices: 18.1 us -> 0.01 us  [shards(): lax.all_gather(values, 'shard', axis=0, tiled=True)]
    all_gather x1, waiting for transfers between devices: 21 us -> 16.2 us  [shards(): lax.all_gather(key_local, 'shard', axis=0, tiled=True)]
    unnamed x29 -> x44, local copies, waits for them, and re-layouts: 11.5 us -> 15.4 us
    all_to_all x1, starting transfers between devices: 18.3 us -> 21.2 us  [shards(): lax.all_to_all(normalized, 'shard', split_axis=1, concat_axis=0, tiled=True)]
  transfers between devices with their start and end apart: 6 -> 12, of which waited for: 5 -> 9; matrix products, arithmetic and copies ran while one was open for 9% -> 9% of each run, Pallas kernels for 0% -> 0%
where the time goes in v1:
time: 267 us; the launch traced here: 266 us
  waiting for transfers between devices  145 us (54%)
  local copies, waits for them, and re-layouts  35.2 us (13%)
  starting transfers between devices  22.5 us (8%)
  matrix products  20.8 us (8%)
  between operations  14.2 us (5%)
  blocking collectives  13.4 us (5%)
  other arithmetic  10.8 us (4%)
  loops' own time  4.19 us (2%)
    ppermute x7, waiting for transfers between devices, turned_line(): parts = [lax.ppermute(parts[0], axis, forward), *parts]  65.1 us
    reduce_scatter x1, waiting for transfers between devices, shards(): lax.psum_scatter(block_terms.reshape(row_count, key_width).astype(jnp.bfl...  32.8 us
    all_to_all x1, waiting for transfers between devices, shards(): lax.all_to_all(normalized, 'shard', split_axis=1, concat_axis=0, tiled=True)  30.7 us
    all_to_all x1, starting transfers between devices, shards(): lax.all_to_all(normalized, 'shard', split_axis=1, concat_axis=0, tiled=True)  21.2 us
    all_gather x1, waiting for transfers between devices, shards(): lax.all_gather(key_local, 'shard', axis=0, tiled=True)  16.2 us
    unnamed x44, local copies, waits for them, and re-layouts  15.4 us
    all_gather x1, blocking collectives, shards(): gain_rows = lax.all_gather(norm_gain, 'shard', axis=0, tiled=True)  13.4 us
    dot_general x3, matrix products, block_scores(): jnp.einsum('tghd,sgd->ghts', query_heads, block_keys, preferred_element_t...  6.61 us
  transfers between devices with their start and end apart: 12, of which 9 were waited for; matrix products, arithmetic and copies ran while one was open for 9% of the time, Pallas kernels for 0%

profile of v1, /device:TPU:0, one launch (start us, length us, event | category | flops | bytes accessed | tf_op | source)
XLA Modules:
  0.0 266.0 jit_solution(5956593594497637627)
XLA Ops:
  7.8 11.1 %collective-permute-done = bf16[512,512]{1,0:T(8,128)(2,1)S(1)} collective-permute-done((bf16[512,512]{1,0:T(8,128)(2,1)}, bf16[512,512]{1,0:T(8,128)(2,1)S(1)}, u32[]{:S(2)}, u32[]{:S(2)}) %collective-permute-start) | collective-permute-done | bytes 524320 | tf_op jit(solution)/shard_map/ppermute | solution.py:19
  18.9 10.4 %collective-permute-done.1 = bf16[512,512]{1,0:T(8,128)(2,1)S(1)} collective-permute-done((bf16[512,512]{1,0:T(8,128)(2,1)S(1)}, bf16[512,512]{1,0:T(8,128)(2,1)S(1)}, u32[]{:S(2)}, u32[]{:S(2)}) %collective-permute-start.1) | collective-permute-done | bytes 524320 | tf_op jit(solution)/shard_map/ppermute | solution.py:19
  29.3 10.4 %collective-permute-done.2 = bf16[512,512]{1,0:T(8,128)(2,1)S(1)} collective-permute-done((bf16[512,512]{1,0:T(8,128)(2,1)S(1)}, bf16[512,512]{1,0:T(8,128)(2,1)S(1)}, u32[]{:S(2)}, u32[]{:S(2)}) %collective-permute-start.2) | collective-permute-done | bytes 524320 | tf_op jit(solution)/shard_map/ppermute | solution.py:19
  39.7 10.4 %collective-permute-done.3 = bf16[512,512]{1,0:T(8,128)(2,1)S(1)} collective-permute-done((bf16[512,512]{1,0:T(8,128)(2,1)S(1)}, bf16[512,512]{1,0:T(8,128)(2,1)S(1)}, u32[]{:S(2)}, u32[]{:S(2)}) %collective-permute-start.3) | collective-permute-done | bytes 524320 | tf_op jit(solution)/shard_map/ppermute | solution.py:19
  50.1 10.4 %collective-permute-done.4 = bf16[512,512]{1,0:T(8,128)(2,1)S(1)} collective-permute-done((bf16[512,512]{1,0:T(8,128)(2,1)S(1)}, bf16[512,512]{1,0:T(8,128)(2,1)S(1)}, u32[]{:S(2)}, u32[]{:S(2)}) %collective-permute-start.4) | collective-permute-done | bytes 524320 | tf_op jit(solution)/shard_map/ppermute | solution.py:19
  60.5 1.7 copy.48
  62.9 13.4 %all-gather = bf16[8,1,512]{2,1,0:T(2,128)(2,1)S(1)} all-gather(bf16[1,1,512]{2,1,0:T(2,128)(2,1)S(1)} %reshape.223), channel_id=1, replica_groups=mesh['replica'=4,'shard'=8] {'shard'}, dimensions={0}, use_global_device_ids=true | all-gather | bytes 9216 | tf_op jit(solution)/shard_map/all_gather | solution.py:71
  76.4 1.6 fusion.48
  78.5 12.4 %collective-permute-done.6 = bf16[512,512]{1,0:T(8,128)(2,1)S(1)} collective-permute-done((bf16[512,512]{1,0:T(8,128)(2,1)}, bf16[512,512]{1,0:T(8,128)(2,1)S(1)}, u32[]{:S(2)}, u32[]{:S(2)}) %collective-permute-start.6) | collective-permute-done | bytes 524320 | tf_op jit(solution)/shard_map/ppermute | solution.py:19
  91.0 1.1 constant_dynamic-update-slice_fusion.15
  92.4 1.2 constant_dynamic-update-slice_fusion.7
  95.2 0.8 copy.44
  97.1 1.0 copy.56
  98.1 1.8 reshape.217
  100.0 2.1 copy.51
  102.0 16.2 %all-gather.5.cloned.1.call-done = bf16[1024,512]{0,1:T(8,128)(2,1)} async-done(((bf16[128,512]{0,1:T(8,128)(2,1)}), bf16[1024,512]{0,1:T(8,128)(2,1)}) %all-gather.5.cloned.1.call-update) | async-done | bytes 1048592 | tf_op jit(solution)/shard_map/all_gather | solution.py:77
  118.2 1.8 reshape.215
  120.1 2.1 copy.49
  122.1 5.1 %while.38 = (s32[]{:T(128)}, f32[4,4,128]{2,1,0:T(4,128)S(1)}, s32[2]{0:T(128)S(1)}, s32[]{:T(128)}, bf16[2,512,4,128]{3,1,2,0:T(8,128)(2,1)}, /*index=5*/bf16[128,4,4,128]{3,0,2,1:T(8,128)(2,1)S(1)}, s32[]{:T(128)}, s32[]{:T(128)}) while((s32[]{:T(128)}, f32[4,4,128]{2,1,0:T(4,128)S(1)}, s32[2]{0:T(128)S(1)}, s32[]{:T(128)}, ...), condition=%wide.region_5.6_spmd.clone, body=%wide.region_1.5_spmd.clone.sunk | while | flops 271647360 | bytes 1219255 | solution.py:110
  123.4 2.6 conditional.9
  124.2 1.8 fusion.6
  127.3 1.1 broadcast_in_dim.78
  128.4 8.9 %while.39 = (s32[]{:T(128)}, f32[4,4,128]{2,1,0:T(4,128)S(1)}, f32[128,4,4,128]{3,0,2,1:T(8,128)}, s32[2]{0:T(128)S(1)}, s32[]{:T(128)}, /*index=5*/bf16[2,512,4...) while((s32[]{:T(128)}, f32[4,4,128]{2,1,0:T(4,128)S(1)}, ...), condition=%wide.region_10.11_spmd.clone, body=%wide.region_6.10_spmd.clone.sunk | while | flops 545587840 | bytes 12311307 | solution.py:133
  129.6 6.4 %conditional.10 = ((f32[4,4,128]{2,1,0:T(4,128)S(1)}, f32[128,4,4,128]{3,0,2,1:T(8,128)})) conditional(s32[]{:T(128)} %convert_element_type.125, (f32[4,4,128]{2,1,0:T(4,128)S(1)}, f32[128,4,4,128]{3,0,2,1:T(8,128)}) %tuple.114, (s32[]{:T(128)}, s32[]{:T(128)}, bf16[2,512,4,128]{3,1,2,0:T(8,128)(2,1)}, s32[]{:T(128)}, ...), branch_computations={%region_7.7_spmd, %region_8.9_spmd} | conditional | flops 545587840 | bytes 12310564 | solution.py:127
  130.4 2.1 fusion.13
  132.6 3.5 %fusion.23 = f32[128,4,4,128]{3,0,2,1:T(8,128)} fusion(f32[128,4,4,128]{3,0,2,1:T(8,128)} %get-tuple-element.259, f32[4,512,128,4]{2,1,3,0:T(8,128)S(1)} %get-tuple-element.552, f32[4,4,128]{2,1,0:T(4,128)S(1)} %get-tuple-element.258, pred[128,512]{0,1:T(8,128)(4,1)S(1)} %broadcast_compare_fusion.1, bf16[2,512,4,128]{3,1,2,0:T(8,128)(2,1)S(1)} %get-tuple-element.260, ...), kind=kOutput, calls=%fused_computation.22 | convolution fusion | flops 272891904 | bytes 6889476 | tf_op jit(solution)/shard_map/while/body/eval_jaxpr/cond/branch_1_fun/ghts,sgd->tghd/dot_general | solution.py:119
  137.3 2.8 %fusion.52 = (f32[4,4,128,128]{3,2,1,0:T(8,128)}, bf16[128,4,4,128]{3,0,2,1:T(8,128)(2,1)}) fusion(f32[128,4,4,128]{3,0,2,1:T(8,128)} %get-tuple-element.306, f32[128,4,4]{0,2,1:T(4,128)S(1)} %bitcast.164), kind=kLoop, calls=%fused_computation.71 | loop fusion | flops 524288 | bytes 2629632
  140.1 2.5 copy.70
  142.6 1.4 multiply_reduce_fusion
  144.0 12.9 %while.40 = (s32[]{:T(128)}, bf16[2,512,4,128]{3,1,2,0:T(8,128)(2,1)}, s32[2]{0:T(128)S(1)}, s32[]{:T(128)}, bf16[1024,512]{0,1:T(8,128)(2,1)}, /*index=5*/bf16[...) while((s32[]{:T(128)}, ...), condition=%wide.region_14.15_spmd.clone, body=%wide.region_11.14_spmd.clone.sunk | while | flops 813236864 | bytes 14842673 | solution.py:173
  145.3 8.6 %conditional.11 = (bf16[1,512,4,128]{3,1,2,0:T(8,128)(2,1)S(1)}) conditional(s32[]{:T(128)} %convert_element_type.126, () %tuple.117, (s32[]{:T(128)}, s32[]{:T(128)}, bf16[1024,512]{0,1:T(8,128)(2,1)}, bf16[128,4,4,128]{3,0,2,1:T(8,128)(2,1)S(1)}, f32[4,4,128]{2,1,0:T(4,128)S(1)}, /*index=5*/f32[4,4,128]{2,1,0:T(4,128)S(1)}, ...), branch_computations={%region_12.12_spmd, %region_13.13_spmd} | conditional | flops 813236864 | bytes 13792822 | solution.py:171
  145.3 1.6 constant_dynamic-slice_fusion
  146.9 2.7 %fusion.55 = f32[4,512,128,4]{2,1,3,0:T(8,128)} fusion(bf16[512,4,128,1]{0,2,3,1:T(8,128)(2,1)S(1)} %bitcast.153, bf16[128,4,4,128]{3,0,2,1:T(8,128)(2,1)S(1)} %get-tuple-element.277), kind=kOutput, calls=%fused_computation.105 | convolution fusion | flops 268435456 | bytes 5242880 | tf_op jit(solution)/shard_map/while/body/eval_jaxpr/cond/branch_1_fun/tghd,sgd->ghts/dot_general | solution.py:86
  149.7 4.2 %fusion.43 = bf16[1,512,4,128]{3,1,2,0:T(8,128)(2,1)S(1)} fusion(bf16[128,4,4,128]{3,0,2,1:T(8,128)(2,1)S(1)} %get-tuple-element.277, f32[4,512,128,4]{2,1,3,0:T(8,128)} %fusion.55, bf16[512,4,128,1]{0,2,3,1:T(8,128)(2,1)S(1)} %bitcast.154, bf16[128,4,4,128]{3,0,2,1:T(8,128)(2,1)} %get-tuple-element.281, f32[4,4,128]{2,1,0:T(4,128)S(1)} %get-tuple-element.282, ...), kind=kOutput, calls=%fused_computation.45 | convolution fusion | flops 544735232 | bytes 6381568 | tf_op jit(solution)/shard_map/while/body/eval_jaxpr/cond/branch_1_fun/ghts,tghd->sgd/dot_general | solution.py:162
  153.9 0.8 constant_dynamic-update-slice_fusion.18
  156.1 0.9 constant_dynamic-update-slice_fusion.18
  156.9 2.1 copy.57
  159.1 1.2 copy.83
  160.5 1.6 copy.82
  162.1 21.2 %all-to-all-start = ((f32[128,8,512]{2,0,1:T(8,128)}), f32[128,8,512]{2,0,1:T(8,128)S(1)}, u32[]{:S(2)}, u32[]{:S(2)}) async-start(f32[128,8,512]{2,0,1:T(8,128)} %bitcast.155), calls=%async_computation | async-start | bytes 4194304 | tf_op jit(solution)/shard_map/all_to_all | solution.py:184
  183.6 32.8 %reduce-scatter.2.cloned.1.call-done = bf16[128,512]{1,0:T(8,128)(2,1)} async-done(((bf16[1024,512]{1,0:T(8,128)(2,1)}), bf16[128,512]{1,0:T(8,128)(2,1)}) %reduce-scatter.2.cloned.1.call-update) | async-done | bytes 131088 | tf_op jit(solution)/shard_map/reduce_scatter | solution.py:174
  216.3 1.0 reshape.222
  218.5 30.7 %all-to-all-done = f32[128,8,512]{2,0,1:T(8,128)S(1)} async-done(((f32[128,8,512]{2,0,1:T(8,128)}), f32[128,8,512]{2,0,1:T(8,128)S(1)}, u32[]{:S(2)}, u32[]{:S(2)}) %all-to-all-start) | async-done | bytes 2097184 | tf_op jit(solution)/shard_map/all_to_all | solution.py:184
  249.2 1.3 fusion.49
  250.5 1.4 copy.52
  251.9 1.2 convert_element_type.77
  253.1 2.0 fusion.50
  255.7 3.8 %subtract_convert_fusion = (bf16[512,512]{1,0:T(8,128)(2,1)}, f32[512,512]{1,0:T(8,128)}) fusion(bf16[512,512]{1,0:T(8,128)(2,1)S(1)} %copy-done.1, bf16[1024,512]{1,0:T(8,128)(2,1)} %fusion.49, bf16[1024,512]{1,0:T(8,128)(2,1)} %all-gather.9.cloned.1.call-done, f32[512,512]{1,0:T(8,128)} %param.26), kind=kOutput, calls=%fused_computation.68 | convolution fusion | flops 538443776 | bytes 5242880 | tf_op jit(solution)/shard_map/td,tk->dk/dot_general | solution.py:187
  (101 shorter events, 12.6 us)
Async XLA Ops:
  7.2 90.9 %all-gather.7.cloned.1.call-start = ((), (), s32[]{:S(2)}) async-start(), calls=%async_computation.3 | async-start | bytes 1179648 | tf_op jit(solution)/shard_map/all_gather | solution.py:78
  7.2 11.6 %collective-permute-start = (bf16[512,512]{1,0:T(8,128)(2,1)}, bf16[512,512]{1,0:T(8,128)(2,1)S(1)}, u32[]{:S(2)}, u32[]{:S(2)}) collective-permute-start(bf16[512,512]{1,0:T(8,128)(2,1)} %param.24), channel_id=1, source_target_pairs={{0,1},{1,2},{2,3},{3,4},{4,5},{5,6},{6,7},{7,0},{8,9},{9,10},{10,1... | collective-permute-start | bytes 1572872 | tf_op jit(solution)/shard_map/ppermute | solution.py:19
  18.9 10.4 %collective-permute-start.1 = (bf16[512,512]{1,0:T(8,128)(2,1)S(1)}, bf16[512,512]{1,0:T(8,128)(2,1)S(1)}, u32[]{:S(2)}, u32[]{:S(2)}) collective-permute-start(bf16[512,512]{1,0:T(8,128)(2,1)S(1)} %collective-permute-done), channel_id=1, source_target_pairs={{0,1},{1,2},{2,3},{3,4},{4,5},{5,6},{6,7},{7,0},{8,9},{9,10},{10,1... | collective-permute-start | bytes 1572872 | tf_op jit(solution)/shard_map/ppermute | solution.py:19
  29.3 10.4 %collective-permute-start.2 = (bf16[512,512]{1,0:T(8,128)(2,1)S(1)}, bf16[512,512]{1,0:T(8,128)(2,1)S(1)}, u32[]{:S(2)}, u32[]{:S(2)}) collective-permute-start(bf16[512,512]{1,0:T(8,128)(2,1)S(1)} %collective-permute-done.1), channel_id=1, source_target_pairs={{0,1},{1,2},{2,3},{3,4},{4,5},{5,6},{6,7},{7,0},{8,9},{9,10},{10,1... | collective-permute-start | bytes 1572872 | tf_op jit(solution)/shard_map/ppermute | solution.py:19
  39.7 10.4 %collective-permute-start.3 = (bf16[512,512]{1,0:T(8,128)(2,1)S(1)}, bf16[512,512]{1,0:T(8,128)(2,1)S(1)}, u32[]{:S(2)}, u32[]{:S(2)}) collective-permute-start(bf16[512,512]{1,0:T(8,128)(2,1)S(1)} %collective-permute-done.2), channel_id=1, source_target_pairs={{0,1},{1,2},{2,3},{3,4},{4,5},{5,6},{6,7},{7,0},{8,9},{9,10},{10,1... | collective-permute-start | bytes 1572872 | tf_op jit(solution)/shard_map/ppermute | solution.py:19
  50.1 10.4 %collective-permute-start.4 = (bf16[512,512]{1,0:T(8,128)(2,1)S(1)}, bf16[512,512]{1,0:T(8,128)(2,1)S(1)}, u32[]{:S(2)}, u32[]{:S(2)}) collective-permute-start(bf16[512,512]{1,0:T(8,128)(2,1)S(1)} %collective-permute-done.3), channel_id=1, source_target_pairs={{0,1},{1,2},{2,3},{3,4},{4,5},{5,6},{6,7},{7,0},{8,9},{9,10},{10,1... | collective-permute-start | bytes 1572872 | tf_op jit(solution)/shard_map/ppermute | solution.py:19
  60.5 17.5 %collective-permute-start.5 = (bf16[512,512]{1,0:T(8,128)(2,1)S(1)}, bf16[512,512]{1,0:T(8,128)(2,1)}, u32[]{:S(2)}, u32[]{:S(2)}) collective-permute-start(bf16[512,512]{1,0:T(8,128)(2,1)S(1)} %collective-permute-done.4), channel_id=1, source_target_pairs={{0,1},{1,2},{2,3},{3,4},{4,5},{5,6},{6,7},{7,0},{8,9},{9,10},{10,1... | collective-permute-start | bytes 1572872 | tf_op jit(solution)/shard_map/ppermute | solution.py:19
  62.2 56.1 %all-gather.5.cloned.1.call-start = ((), (), s32[]{:S(2)}) async-start(), calls=%async_computation.2 | async-start | bytes 1179648 | tf_op jit(solution)/shard_map/all_gather | solution.py:77
  76.4 15.9 %copy-start.1 = (bf16[512,512]{1,0:T(8,128)(2,1)S(1)}, bf16[512,512]{1,0:T(8,128)(2,1)}, u32[]{:S(2)}) copy-start(bf16[512,512]{1,0:T(8,128)(2,1)} %param.24) | copy-start | bytes 1572868
  78.0 13.0 %collective-permute-start.6 = (bf16[512,512]{1,0:T(8,128)(2,1)}, bf16[512,512]{1,0:T(8,128)(2,1)S(1)}, u32[]{:S(2)}, u32[]{:S(2)}) collective-permute-start(bf16[512,512]{1,0:T(8,128)(2,1)} %collective-permute-done.5), channel_id=1, source_target_pairs={{0,1},{1,2},{2,3},{3,4},{4,5},{5,6},{6,7},{7,0},{8,9},{9,10},{10,1... | collective-permute-start | bytes 1572872 | tf_op jit(solution)/shard_map/ppermute | solution.py:19
  92.3 1.5 copy-start.2
  93.8 2.4 copy-start.5
  93.8 3.0 %copy-start.6 = (bf16[128,2048]{1,0:T(8,128)(2,1)S(1)}, bf16[128,2048]{1,0:T(8,128)(2,1)}, u32[]{:S(2)}) copy-start(bf16[128,2048]{1,0:T(8,128)(2,1)} %param.23) | copy-start | bytes 1572868
  96.0 120.3 %reduce-scatter.2.cloned.1.call-start = ((), (), s32[]{:S(2)}) async-start(), calls=%async_computation.4 | async-start | bytes 1179648 | tf_op jit(solution)/shard_map/reduce_scatter | solution.py:174
  122.1 6.2 %copy-start.4 = (bf16[2,512,4,128]{3,1,2,0:T(8,128)(2,1)S(1)}, bf16[2,512,4,128]{3,1,2,0:T(8,128)(2,1)}, u32[]{:S(2)}) copy-start(bf16[2,512,4,128]{3,1,2,0:T(8,128)(2,1)} %copy.51) | copy-start | bytes 3145732
  137.3 6.7 %copy-start = (bf16[1024,512]{0,1:T(8,128)(2,1)S(1)}, bf16[1024,512]{0,1:T(8,128)(2,1)}, u32[]{:S(2)}) copy-start(bf16[1024,512]{0,1:T(8,128)(2,1)} %all-gather.7.cloned.1.call-done) | copy-start | bytes 3145732
  156.9 3.3 %copy-start.3 = (bf16[128,4096]{1,0:T(8,128)(2,1)S(1)}, bf16[128,4096]{1,0:T(8,128)(2,1)}, u32[]{:S(2)}) copy-start(bf16[128,4096]{1,0:T(8,128)(2,1)} %param.20) | copy-start | bytes 3145732
  162.1 56.4 %copy-start.7 = (bf16[512]{0:T(512)(128)(2,1)S(1)}, bf16[512]{0:T(512)(128)(2,1)}, u32[]{:S(2)}) copy-start(bf16[512]{0:T(512)(128)(2,1)} %param.25) | copy-start | bytes 3076
  162.1 87.1 %all-to-all-start = ((f32[128,8,512]{2,0,1:T(8,128)}), f32[128,8,512]{2,0,1:T(8,128)S(1)}, u32[]{:S(2)}, u32[]{:S(2)}) async-start(f32[128,8,512]{2,0,1:T(8,128)} %bitcast.155), calls=%async_computation | async-start | bytes 4194304 | tf_op jit(solution)/shard_map/all_to_all | solution.py:184
  183.3 69.8 %all-gather.9.cloned.1.call-start = ((), (), s32[]{:S(2)}) async-start(), calls=%async_computation.5 | async-start | bytes 1179648 | tf_op jit(solution)/shard_map/all_gather | solution.py:186
  218.5 36.6 %copy-start.8 = (f32[512]{0:T(512)S(1)}, f32[512]{0:T(512)}, u32[]{:S(2)}) copy-start(f32[512]{0:T(512)} %param.27) | copy-start | bytes 6148
Sparse Core Ops, SparseCore 0:
  62.3 30.6 all-gather.6
  96.1 22.0 all-gather.4
  160.4 55.9 reduce-scatter.1
  218.6 27.5 all-gather.8
